TPU v7x, 32 devices: a whole 2x2x4 slice. The times are simulated.
32 devices in a mesh: chan: 8 (over z, y), win: 4 (over x, core).
Axes of the slice: x: 2, y: 2, z: 4, core: 2. Of those that a mesh axis runs over, the one named last changes fastest.
Arguments:
- samples: bfloat16 [8, 256, 6144], P('win', 'chan'), may hold values from -6 to 6
- pair_offsets: int32 [8, 3], P('chan'), may hold values from 0 to 2, each once within a row
- spectral_slot_position: int32 [1024], replicated, may hold values from 1 to 3071, as said below
Outputs:
- correlations: float32 [256, 3, 2, 32, 1024], P('chan', None, None, None, 'win')
Inputs may be any that keep to these rules, and one draw needn't show every extreme that they name: `pair_offsets`: each row holds every offset of 0 to 2 once. `spectral_slot_position`: distinct and rising; the first is 1 and the last is 3071.
All inputs are finite; a program needn't handle non-finite values.
Results may differ from a plain program's by a relative error of at most 0.0036.
Values sent between devices are 32-bit elements; how exact they have to be, the bound alone decides.
No kernel may reach another device: no remote copies, remote signals or barrier semaphores. Data moves between devices by JAX's collectives and lax.ppermute only.
A program may use at most 64 MiB of HBM per device.

v0:
```python
import math
import jax
import jax.numpy as jnp
from jax import lax
from jax.sharding import PartitionSpec as P

S = 6144
HALF = 64
TB = 1024
EPSILON = 1e-06


def passed_along(value, axis, steps):
    count = lax.axis_size(axis)
    leading, last = (max(0, -steps), min(count, count - steps))
    return lax.ppermute(value, axis, [(source, source + steps) for source in range(leading, last)])


def angle_parts(spectral_slot_position):
    factor = 2.0 * math.pi / S
    moments = jnp.arange(TB, dtype=jnp.int32)
    base = (moments[:, None] * spectral_slot_position[None, :] % S).astype(jnp.float32) * factor
    starts = jnp.arange(S // TB, dtype=jnp.int32) * TB
    turns = (starts[:, None] * spectral_slot_position[None, :] % S).astype(jnp.float32) * factor
    return (jnp.cos(base), jnp.sin(base), jnp.cos(turns), jnp.sin(turns))


def block_table(base_cos, base_sin, turn_cos, turn_sin):
    scale = 1.0 / math.sqrt(S)
    cos_part = (base_cos * turn_cos - base_sin * turn_sin) * scale
    sin_part = (base_sin * turn_cos + base_cos * turn_sin) * scale
    return jnp.concatenate([cos_part, sin_part], axis=-1).astype(jnp.bfloat16)


def whiten(spectra, half_width):
    freq_count = spectra.shape[-1]
    powers = spectra[..., 0, :] * spectra[..., 0, :] + spectra[..., 1, :] * spectra[..., 1, :]
    places = jnp.arange(freq_count, dtype=jnp.int32)
    banded = (jnp.abs(places[:, None] - places[None, :]) <= half_width).astype(jnp.float32)
    tallies = jnp.sum(banded, axis=0)
    flattened = powers.reshape(-1, freq_count)
    smoothed_amplitude = (
        jnp.dot(flattened, banded, precision=lax.Precision.HIGHEST).reshape(powers.shape) / tallies
    )
    amplitude = jnp.sqrt(smoothed_amplitude + EPSILON)
    return spectra / amplitude[..., None, :]


def arrange(field):
    win_count, chan_count, _, freq_count = field.shape
    return field.transpose(3, 1, 0, 2).reshape(freq_count, chan_count, win_count * 2)


def pair_blocks(spectra, offsets, windows):
    nearer = passed_along(spectra, "chan", 1)
    farther = passed_along(spectra, "chan", 2)
    win_count, chan_count, _, freq_count = spectra.shape
    flipped = jnp.stack([spectra[:, :, 1], -spectra[:, :, 0]], axis=2)
    left = jnp.concatenate([arrange(spectra), arrange(flipped)], axis=1)
    right = jnp.concatenate([arrange(spectra), arrange(nearer), arrange(farther)], axis=1)
    joined = jnp.einsum("fik,fjk->fij", left, right, precision=lax.Precision.HIGHEST) / windows
    joined = joined.reshape(freq_count, 2, chan_count, 3, chan_count)
    slots = []
    for position in range(offsets.shape[0]):
        chosen = offsets[position]
        slots.append(
            jnp.where(
                chosen == 0,
                joined[:, :, :, 0],
                jnp.where(chosen == 1, joined[:, :, :, 1], joined[:, :, :, 2]),
            )
        )
    stacked = jnp.stack(slots, axis=0)
    return stacked.transpose(3, 0, 2, 4, 1)


def shards(samples, pair_offsets, spectral_slot_position):
    win_count, sensor_total, segment_span = samples.shape
    freq_count = spectral_slot_position.shape[0]
    time_series = samples.reshape(win_count * sensor_total, segment_span)
    base_cos, base_sin, turn_cos, turn_sin = angle_parts(spectral_slot_position)

    def add_block(step, total):
        piece = lax.dynamic_slice_in_dim(time_series, step * TB, TB, 1)
        row_cos = lax.dynamic_slice_in_dim(turn_cos, step, 1, 0)
        row_sin = lax.dynamic_slice_in_dim(turn_sin, step, 1, 0)
        table = block_table(base_cos, base_sin, row_cos, row_sin)
        return total + jnp.dot(piece, table, preferred_element_type=jnp.float32)

    initial = jnp.zeros((win_count * sensor_total, 2 * freq_count), jnp.float32)
    raw_parts = lax.fori_loop(0, segment_span // TB, add_block, initial)
    spectra = jnp.stack([raw_parts[:, :freq_count], -raw_parts[:, freq_count:]], axis=1)
    spectra = spectra.reshape(win_count, sensor_total, 2, freq_count)
    whitened = whiten(spectra, HALF)
    offsets = pair_offsets[0]
    slabs = lax.all_to_all(whitened, "win", split_axis=3, concat_axis=0, tiled=True)
    return pair_blocks(slabs, offsets, slabs.shape[0])


def solution(mesh):
    in_specs = (P("win", "chan", None), P("chan", None), P())
    out_specs = P("chan", None, None, None, "win")
    return jax.shard_map(shards, mesh=mesh, in_specs=in_specs, out_specs=out_specs, check_vma=False)
```

profile of v0, /device:TPU:28, one launch (start us, length us, event | category | flops | bytes accessed | tf_op | source)
XLA Modules:
  0.0 227.4 jit_solution(14979115997876258393)
XLA Ops:
  1.1 138.7 %while.16 = (s32[]{:T(128)}, f32[64,2048]{1,0:T(8,128)S(1)}, bf16[64,6144]{1,0:T(8,128)(2,1)}, f32[6,1024]{1,0:T(8,128)S(1)}, f32[6,1024]{1,0:T(8,128)S(1)}, /*i...) while((s32[]{:T(128)}, f32[64,2048]{1,0:T(8,128)S(1)}, ...), condition=%wide.region_1.2_spmd.clone.clone.clone, body=%wide.region_0.1_spmd.clone.clone.clone.sunk | while | flops 297009152 | bytes 9597093 | solution.py:91
  1.2 20.5 %fusion.73 = (bf16[1024,1024]{1,0:T(8,128)(2,1)S(1)}, bf16[1024,1024]{1,0:T(8,128)(2,1)}) fusion(s32[1024]{0:T(1024)} %get-tuple-element.293, f32[1024]{0:T(1024)S(1)} %bitcast.88, f32[1024]{0:T(1024)S(1)} %bitcast.89), kind=kLoop, calls=%fused_computation.20.clone.1 | loop fusion | flops 19922944 | bytes 4206592 | tf_op jit(solution)/shard_map/convert
  21.7 2.6 %fusion.74 = f32[64,2048]{1,0:T(8,128)S(1)} fusion(bf16[1024,1024]{1,0:T(8,128)(2,1)} %get-tuple-element.266, bf16[1024,1024]{1,0:T(8,128)(2,1)S(1)} %get-tuple-element.267, f32[64,2048]{1,0:T(8,128)S(1)} %get-tuple-element.279, pred[]{:T(512)S(6)} %compare.5, bf16[64,6144]{1,0:T(8,128)(2,1)} %get-tuple-element.290, s32[]{:T(128)S(6)} %select_n.219), kind=kOutput, calls=%fused_computation.25.clone.1 | convolution fusion | flops 277086208 | bytes 5373957 | tf_op jit(solution)/shard_map/while/body/eval_jaxpr/dot_general | solution.py:88
  24.3 20.5 %fusion.73 = (bf16[1024,1024]{1,0:T(8,128)(2,1)S(1)}, bf16[1024,1024]{1,0:T(8,128)(2,1)}) fusion(s32[1024]{0:T(1024)} %get-tuple-element.293, f32[1024]{0:T(1024)S(1)} %bitcast.88, f32[1024]{0:T(1024)S(1)} %bitcast.89), kind=kLoop, calls=%fused_computation.20.clone.1 | loop fusion | flops 19922944 | bytes 4206592 | tf_op jit(solution)/shard_map/convert
  44.8 2.6 %fusion.74 = f32[64,2048]{1,0:T(8,128)S(1)} fusion(bf16[1024,1024]{1,0:T(8,128)(2,1)} %get-tuple-element.266, bf16[1024,1024]{1,0:T(8,128)(2,1)S(1)} %get-tuple-element.267, f32[64,2048]{1,0:T(8,128)S(1)} %get-tuple-element.279, pred[]{:T(512)S(6)} %compare.5, bf16[64,6144]{1,0:T(8,128)(2,1)} %get-tuple-element.290, s32[]{:T(128)S(6)} %select_n.219), kind=kOutput, calls=%fused_computation.25.clone.1 | convolution fusion | flops 277086208 | bytes 5373957 | tf_op jit(solution)/shard_map/while/body/eval_jaxpr/dot_general | solution.py:88
  47.4 20.5 %fusion.73 = (bf16[1024,1024]{1,0:T(8,128)(2,1)S(1)}, bf16[1024,1024]{1,0:T(8,128)(2,1)}) fusion(s32[1024]{0:T(1024)} %get-tuple-element.293, f32[1024]{0:T(1024)S(1)} %bitcast.88, f32[1024]{0:T(1024)S(1)} %bitcast.89), kind=kLoop, calls=%fused_computation.20.clone.1 | loop fusion | flops 19922944 | bytes 4206592 | tf_op jit(solution)/shard_map/convert
  67.9 2.6 %fusion.74 = f32[64,2048]{1,0:T(8,128)S(1)} fusion(bf16[1024,1024]{1,0:T(8,128)(2,1)} %get-tuple-element.266, bf16[1024,1024]{1,0:T(8,128)(2,1)S(1)} %get-tuple-element.267, f32[64,2048]{1,0:T(8,128)S(1)} %get-tuple-element.279, pred[]{:T(512)S(6)} %compare.5, bf16[64,6144]{1,0:T(8,128)(2,1)} %get-tuple-element.290, s32[]{:T(128)S(6)} %select_n.219), kind=kOutput, calls=%fused_computation.25.clone.1 | convolution fusion | flops 277086208 | bytes 5373957 | tf_op jit(solution)/shard_map/while/body/eval_jaxpr/dot_general | solution.py:88
  70.5 20.5 %fusion.73 = (bf16[1024,1024]{1,0:T(8,128)(2,1)S(1)}, bf16[1024,1024]{1,0:T(8,128)(2,1)}) fusion(s32[1024]{0:T(1024)} %get-tuple-element.293, f32[1024]{0:T(1024)S(1)} %bitcast.88, f32[1024]{0:T(1024)S(1)} %bitcast.89), kind=kLoop, calls=%fused_computation.20.clone.1 | loop fusion | flops 19922944 | bytes 4206592 | tf_op jit(solution)/shard_map/convert
  91.0 2.6 %fusion.74 = f32[64,2048]{1,0:T(8,128)S(1)} fusion(bf16[1024,1024]{1,0:T(8,128)(2,1)} %get-tuple-element.266, bf16[1024,1024]{1,0:T(8,128)(2,1)S(1)} %get-tuple-element.267, f32[64,2048]{1,0:T(8,128)S(1)} %get-tuple-element.279, pred[]{:T(512)S(6)} %compare.5, bf16[64,6144]{1,0:T(8,128)(2,1)} %get-tuple-element.290, s32[]{:T(128)S(6)} %select_n.219), kind=kOutput, calls=%fused_computation.25.clone.1 | convolution fusion | flops 277086208 | bytes 5373957 | tf_op jit(solution)/shard_map/while/body/eval_jaxpr/dot_general | solution.py:88
  93.7 20.5 %fusion.73 = (bf16[1024,1024]{1,0:T(8,128)(2,1)S(1)}, bf16[1024,1024]{1,0:T(8,128)(2,1)}) fusion(s32[1024]{0:T(1024)} %get-tuple-element.293, f32[1024]{0:T(1024)S(1)} %bitcast.88, f32[1024]{0:T(1024)S(1)} %bitcast.89), kind=kLoop, calls=%fused_computation.20.clone.1 | loop fusion | flops 19922944 | bytes 4206592 | tf_op jit(solution)/shard_map/convert
  114.2 2.6 %fusion.74 = f32[64,2048]{1,0:T(8,128)S(1)} fusion(bf16[1024,1024]{1,0:T(8,128)(2,1)} %get-tuple-element.266, bf16[1024,1024]{1,0:T(8,128)(2,1)S(1)} %get-tuple-element.267, f32[64,2048]{1,0:T(8,128)S(1)} %get-tuple-element.279, pred[]{:T(512)S(6)} %compare.5, bf16[64,6144]{1,0:T(8,128)(2,1)} %get-tuple-element.290, s32[]{:T(128)S(6)} %select_n.219), kind=kOutput, calls=%fused_computation.25.clone.1 | convolution fusion | flops 277086208 | bytes 5373957 | tf_op jit(solution)/shard_map/while/body/eval_jaxpr/dot_general | solution.py:88
  116.8 20.5 %fusion.73 = (bf16[1024,1024]{1,0:T(8,128)(2,1)S(1)}, bf16[1024,1024]{1,0:T(8,128)(2,1)}) fusion(s32[1024]{0:T(1024)} %get-tuple-element.293, f32[1024]{0:T(1024)S(1)} %bitcast.88, f32[1024]{0:T(1024)S(1)} %bitcast.89), kind=kLoop, calls=%fused_computation.20.clone.1 | loop fusion | flops 19922944 | bytes 4206592 | tf_op jit(solution)/shard_map/convert
  137.3 2.6 %fusion.74 = f32[64,2048]{1,0:T(8,128)S(1)} fusion(bf16[1024,1024]{1,0:T(8,128)(2,1)} %get-tuple-element.266, bf16[1024,1024]{1,0:T(8,128)(2,1)S(1)} %get-tuple-element.267, f32[64,2048]{1,0:T(8,128)S(1)} %get-tuple-element.279, pred[]{:T(512)S(6)} %compare.5, bf16[64,6144]{1,0:T(8,128)(2,1)} %get-tuple-element.290, s32[]{:T(128)S(6)} %select_n.219), kind=kOutput, calls=%fused_computation.25.clone.1 | convolution fusion | flops 277086208 | bytes 5373957 | tf_op jit(solution)/shard_map/while/body/eval_jaxpr/dot_general | solution.py:88
  142.2 2.2 reshape.161
  144.5 11.4 %all_to_all.18 = f32[4,1,32768]{2,1,0:T(1,128)S(1)} all-to-all(f32[4,1,32768]{2,1,0:T(1,128)S(1)} %reshape.161), channel_id=1, replica_groups=mesh['chan'=8,'win'=4] {'win'}, dimensions={0} | all-to-all | bytes 1048576 | tf_op jit(solution)/shard_map/all_to_all | solution.py:96
  168.4 2.3 copy.38
  172.1 4.4 %collective-permute-done = f32[8,32,2,256]{3,1,2,0:T(8,128)} collective-permute-done((f32[8,32,2,256]{3,1,2,0:T(8,128)S(1)}, f32[8,32,2,256]{3,1,2,0:T(8,128)}, u32[]{:S(2)}, u32[]{:S(2)}) %collective-permute-start) | collective-permute-done | bytes 524320 | tf_op jit(solution)/shard_map/ppermute | solution.py:16
  176.5 3.9 %copy.39 = f32[256,32,8,2]{1,3,2,0:T(2,128)} copy(f32[256,32,8,2]{0,1,3,2:T(8,128)} %bitcast.13) | data formatting | bytes 1048576 | tf_op jit(solution)/shard_map/transpose | solution.py:51
  180.4 7.1 %collective-permute-done.1 = f32[8,32,2,256]{3,1,2,0:T(8,128)S(1)} collective-permute-done((f32[8,32,2,256]{3,1,2,0:T(8,128)S(1)}, f32[8,32,2,256]{3,1,2,0:T(8,128)S(1)}, u32[]{:S(2)}, u32[]{:S(2)}) %collective-permute-start.1) | collective-permute-done | bytes 524320 | tf_op jit(solution)/shard_map/ppermute | solution.py:16
  187.6 2.4 %copy.40 = f32[256,32,8,2]{1,3,2,0:T(2,128)} copy(f32[256,32,8,2]{0,1,3,2:T(8,128)S(1)} %bitcast.87) | data formatting | bytes 1048576 | tf_op jit(solution)/shard_map/transpose | solution.py:51
  190.0 18.9 %broadcast_multiply_fusion = f32[256,64,96]{2,1,0:T(8,128)} fusion(f32[256,32,16]{1,2,0:T(8,128)} %bitcast.76, f32[256,32,16]{1,2,0:T(8,128)S(1)} %bitcast.75, f32[256,32,16]{1,2,0:T(8,128)} %bitcast.78, f32[256,32,16]{1,2,0:T(8,128)} %bitcast.77), kind=kOutput, calls=%fused_computation.32 | convolution fusion | flops 304611328 | bytes 8388608 | tf_op jit(solution)/shard_map/fik,fjk->fij/dot_general | solution.py:61
  208.9 8.5 %copy.41 = f32[256,64,96]{0,2,1:T(8,128)} copy(f32[256,64,96]{2,1,0:T(8,128)} %broadcast_multiply_fusion) | data formatting | bytes 12582912 | tf_op jit(solution)/shard_map/div | solution.py:61
  217.4 3.7 %select_bitcast_fusion = f32[1,256,2,32,32]{1,4,3,2,0:T(8,128)S(1)} fusion(f32[256,2,32,3,32]{0,4,3,2,1:T(8,128)} %bitcast.73, pred[]{:T(512)} %bitcast.27, pred[]{:T(512)} %bitcast.25), kind=kLoop, calls=%fused_computation.51 | loop fusion | flops 1048576 | bytes 8388610 | tf_op jit(solution)/shard_map/jit(_where)/select_n | solution.py:67
  223.9 3.5 %copy.48 = f32[32,3,2,32,256]{4,3,2,1,0:T(8,128)} copy(f32[32,3,2,32,256]{4,3,0,2,1:T(8,128)S(1)} %maximum_bitcast_fusion) | data formatting | bytes 12582912 | tf_op jit(solution)/shard_map/transpose | solution.py:74
  (30 shorter events, 16.6 us)
Async XLA Ops:
  144.5 19.5 %copy-start.1 = (s32[1,3]{1,0:T(1,128)S(1)}, s32[1,3]{1,0:T(1,128)}, u32[]{:S(2)}) copy-start(s32[1,3]{1,0:T(1,128)} %param.6) | copy-start | bytes 40
  161.2 15.3 %collective-permute-start = (f32[8,32,2,256]{3,1,2,0:T(8,128)S(1)}, f32[8,32,2,256]{3,1,2,0:T(8,128)}, u32[]{:S(2)}, u32[]{:S(2)}) collective-permute-start(f32[8,32,2,256]{3,1,2,0:T(8,128)S(1)} %bitcast.81), channel_id=1, source_target_pairs={{0,4},{4,8},{8,12},{12,16},{16,20},{20,24},{24,28},{1,5},{5,9},{9,... | collective-permute-start | bytes 1572872 | tf_op jit(solution)/shard_map/ppermute | solution.py:16
  162.5 25.1 %collective-permute-start.1 = (f32[8,32,2,256]{3,1,2,0:T(8,128)S(1)}, f32[8,32,2,256]{3,1,2,0:T(8,128)S(1)}, u32[]{:S(2)}, u32[]{:S(2)}) collective-permute-start(f32[8,32,2,256]{3,1,2,0:T(8,128)S(1)} %bitcast.82), channel_id=1, source_target_pairs={{0,8},{4,12},{8,16},{12,20},{16,24},{20,28},{1,9},{5,13},{9,17},{1... | collective-permute-start | bytes 1572872 | tf_op jit(solution)/shard_map/ppermute | solution.py:16
  217.4 4.7 %copy-start = (f32[256,64,96]{0,2,1:T(8,128)S(1)}, f32[256,64,96]{0,2,1:T(8,128)}, u32[]{:S(2)}) copy-start(f32[256,64,96]{0,2,1:T(8,128)} %copy.41) | copy-start | bytes 18874372
where the time goes:
time: 228 us; the launch traced here: 227 us
  other arithmetic  132 us (58%)
  matrix products  35.3 us (15%)
  local copies, waits for them, and re-layouts  30.5 us (13%)
  waiting for transfers between devices  11.5 us (5%)
  blocking collectives  11.4 us (5%)
  between operations  3.83 us (2%)
  starting transfers between devices  2.76 us (1%)
    another operation x6, other arithmetic  123 us
    dot_general x1, matrix products, pair_blocks(): jnp.einsum('fik,fjk->fij', left, right, precision=lax.Precision.HIGHEST)  18.9 us
    dot_general x6, matrix products, add_block(): return total + jnp.dot(piece, table, preferred_element_type=jnp.float32)  15.5 us
    ppermute x2, waiting for transfers between devices, passed_along(): lax.ppermute(value, axis, [(source, source + steps) for source in range(l...  11.5 us
    all_to_all x1, blocking collectives, shards(): lax.all_to_all(whitened, 'win', split_axis=3, concat_axis=0, tiled=True)  11.4 us
    transpose x4, local copies, waits for them, and re-layouts, arrange(): field.transpose(3, 1, 0, 2).reshape(freq_count, chan_count, win_count * 2)  10.1 us
    div x1, local copies, waits for them, and re-layouts, pair_blocks(): jnp.einsum('fik,fjk->fij', left, right, precision=lax.Precision.HIGHEST)  8.54 us
    unnamed x6, local copies, waits for them, and re-layouts  4.95 us
  transfers between devices with their start and end apart: 2, of which 2 were waited for; matrix products, arithmetic and copies ran while one was open for 4% of the time, Pallas kernels for 0%

commit v1 on v0

--- a/solution.py
+++ b/solution.py
@@ -3,11 +3,26 @@
 import jax.numpy as jnp
 from jax import lax
 from jax.sharding import PartitionSpec as P
+from jax.lax import axis_index, axis_size, ppermute
 
 S = 6144
 HALF = 64
 TB = 1024
 EPSILON = 1e-06
+
+
+def _track_frames(raw, d0, local_block):
+    e_now = raw.shape
+    known = raw.reshape(*e_now[:d0], local_block, e_now[d0] // local_block, *e_now[d0 + 1 :])
+    return jnp.moveaxis(known, d0, 0)
+
+
+def extend_indices(m, axis_no):
+    m = jnp.moveaxis(m, 0, axis_no)
+    e_next = m.shape
+    return m.reshape(
+        *e_next[:axis_no], e_next[axis_no] * e_next[axis_no + 1], *e_next[axis_no + 2 :]
+    )
 
 
 def passed_along(value, axis, steps):
@@ -93,7 +108,24 @@
     spectra = spectra.reshape(win_count, sensor_total, 2, freq_count)
     whitened = whiten(spectra, HALF)
     offsets = pair_offsets[0]
-    slabs = lax.all_to_all(whitened, "win", split_axis=3, concat_axis=0, tiled=True)
+
+    def update_values(message, mesh_name, v0, values):
+        all_values = axis_size(mesh_name)
+        mixed_arr = axis_index(mesh_name)
+        piece_next, lower = (all_values, mixed_arr)
+        a_now = _track_frames(message, v0, piece_next)
+        odd = a_now
+        t = 1
+        while t < piece_next:
+            w1, extra = ((lower + t) % piece_next, (lower - t) % piece_next)
+            a_next = lax.dynamic_index_in_dim(a_now, w1, 0)
+            front = tuple(((no, (no + t) % piece_next) for no in range(piece_next)))
+            top = ppermute(a_next, axis_name=mesh_name, perm=front)
+            odd = lax.dynamic_update_slice_in_dim(odd, top, extra, axis=0)
+            t += 1
+        return extend_indices(odd, values)
+
+    slabs = update_values(whitened, "win", 3, values=0)
     return pair_blocks(slabs, offsets, slabs.shape[0])
 
 

time: 228 us -> 218 us (0.956)
  blocking collectives: 11.4 us -> 0 us
  local copies, waits for them, and re-layouts: 30.5 us -> 24.2 us
  waiting for transfers between devices: 11.5 us -> 17.2 us
  starting transfers between devices: 2.76 us -> 5.76 us
    all_to_all x1 -> x0, blocking collectives: 11.4 us -> none  [shards(): lax.all_to_all(whitened, 'win', split_axis=3, concat_axis=0, tiled=True)]
    ppermute x0 -> x3, waiting for transfers between devices: none -> 4.5 us  [update_values(): top = ppermute(a_next, axis_name=mesh_name, perm=front)]
    unnamed x6 -> x4, local copies, waits for them, and re-layouts: 4.95 us -> 0.93 us
    ppermute x0 -> x3, starting transfers between devices: none -> 3 us  [update_values(): top = ppermute(a_next, axis_name=mesh_name, perm=front)]
  transfers between devices with their start and end apart: 2 -> 5, of which waited for: 2 -> 5; matrix products, arithmetic and copies ran while one was open for 4% -> 4% of each run, Pallas kernels for 0% -> 0%
where the time goes in v1:
time: 218 us; the launch traced here: 217 us
  other arithmetic  130 us (60%)
  matrix products  35.3 us (16%)
  local copies, waits for them, and re-layouts  24.2 us (11%)
  waiting for transfers between devices  17.2 us (8%)
  starting transfers between devices  5.76 us (3%)
  between operations  4.02 us (2%)
    another operation x6, other arithmetic  123 us
    dot_general x1, matrix products, pair_blocks(): jnp.einsum('fik,fjk->fij', left, right, precision=lax.Precision.HIGHEST)  18.9 us
    dot_general x6, matrix products, add_block(): return total + jnp.dot(piece, table, preferred_element_type=jnp.float32)  15.5 us
    ppermute x2, waiting for transfers between devices, passed_along(): lax.ppermute(value, axis, [(source, source + steps) for source in range(l...  12.7 us
    transpose x4, local copies, waits for them, and re-layouts, arrange(): field.transpose(3, 1, 0, 2).reshape(freq_count, chan_count, win_count * 2)  10.1 us
    div x1, local copies, waits for them, and re-layouts, pair_blocks(): jnp.einsum('fik,fjk->fij', left, right, precision=lax.Precision.HIGHEST)  8.54 us
    ppermute x3, waiting for transfers between devices, update_values(): top = ppermute(a_next, axis_name=mesh_name, perm=front)  4.5 us
    select_n x2, other arithmetic, pair_blocks(): jnp.where(chosen == 0, joined[:, :, :, 0], jnp.where(chosen == 1, joined[...  4.45 us
  transfers between devices with their start and end apart: 5, of which 5 were waited for; matrix products, arithmetic and copies ran while one was open for 4% of the time, Pallas kernels for 0%

profile of v1, /device:TPU:28, one launch (start us, length us, event | category | flops | bytes accessed | tf_op | source)
XLA Modules:
  0.0 216.6 jit_solution(10973134920219353543)
XLA Ops:
  1.1 138.7 %while.16 = (s32[]{:T(128)}, f32[64,2048]{1,0:T(8,128)S(1)}, bf16[64,6144]{1,0:T(8,128)(2,1)}, f32[6,1024]{1,0:T(8,128)S(1)}, f32[6,1024]{1,0:T(8,128)S(1)}, /*i...) while((s32[]{:T(128)}, f32[64,2048]{1,0:T(8,128)S(1)}, ...), condition=%wide.region_1.2_spmd.clone.clone.clone, body=%wide.region_0.1_spmd.clone.clone.clone.sunk | while | flops 297009152 | bytes 9597093 | solution.py:106
  1.2 20.5 %fusion.74 = (bf16[1024,1024]{1,0:T(8,128)(2,1)S(1)}, bf16[1024,1024]{1,0:T(8,128)(2,1)}) fusion(s32[1024]{0:T(1024)} %get-tuple-element.296, f32[1024]{0:T(1024)S(1)} %bitcast.91, f32[1024]{0:T(1024)S(1)} %bitcast.92), kind=kLoop, calls=%fused_computation.20.clone.1 | loop fusion | flops 19922944 | bytes 4206592 | tf_op jit(solution)/shard_map/convert
  21.7 2.6 %fusion.75 = f32[64,2048]{1,0:T(8,128)S(1)} fusion(bf16[1024,1024]{1,0:T(8,128)(2,1)} %get-tuple-element.269, bf16[1024,1024]{1,0:T(8,128)(2,1)S(1)} %get-tuple-element.270, f32[64,2048]{1,0:T(8,128)S(1)} %get-tuple-element.282, pred[]{:T(512)S(6)} %compare.11, bf16[64,6144]{1,0:T(8,128)(2,1)} %get-tuple-element.293, s32[]{:T(128)S(6)} %select_n.276), kind=kOutput, calls=%fused_computation.25.clone.1 | convolution fusion | flops 277086208 | bytes 5373957 | tf_op jit(solution)/shard_map/while/body/eval_jaxpr/dot_general | solution.py:103
  24.3 20.5 %fusion.74 = (bf16[1024,1024]{1,0:T(8,128)(2,1)S(1)}, bf16[1024,1024]{1,0:T(8,128)(2,1)}) fusion(s32[1024]{0:T(1024)} %get-tuple-element.296, f32[1024]{0:T(1024)S(1)} %bitcast.91, f32[1024]{0:T(1024)S(1)} %bitcast.92), kind=kLoop, calls=%fused_computation.20.clone.1 | loop fusion | flops 19922944 | bytes 4206592 | tf_op jit(solution)/shard_map/convert
  44.8 2.6 %fusion.75 = f32[64,2048]{1,0:T(8,128)S(1)} fusion(bf16[1024,1024]{1,0:T(8,128)(2,1)} %get-tuple-element.269, bf16[1024,1024]{1,0:T(8,128)(2,1)S(1)} %get-tuple-element.270, f32[64,2048]{1,0:T(8,128)S(1)} %get-tuple-element.282, pred[]{:T(512)S(6)} %compare.11, bf16[64,6144]{1,0:T(8,128)(2,1)} %get-tuple-element.293, s32[]{:T(128)S(6)} %select_n.276), kind=kOutput, calls=%fused_computation.25.clone.1 | convolution fusion | flops 277086208 | bytes 5373957 | tf_op jit(solution)/shard_map/while/body/eval_jaxpr/dot_general | solution.py:103
  47.4 20.5 %fusion.74 = (bf16[1024,1024]{1,0:T(8,128)(2,1)S(1)}, bf16[1024,1024]{1,0:T(8,128)(2,1)}) fusion(s32[1024]{0:T(1024)} %get-tuple-element.296, f32[1024]{0:T(1024)S(1)} %bitcast.91, f32[1024]{0:T(1024)S(1)} %bitcast.92), kind=kLoop, calls=%fused_computation.20.clone.1 | loop fusion | flops 19922944 | bytes 4206592 | tf_op jit(solution)/shard_map/convert
  67.9 2.6 %fusion.75 = f32[64,2048]{1,0:T(8,128)S(1)} fusion(bf16[1024,1024]{1,0:T(8,128)(2,1)} %get-tuple-element.269, bf16[1024,1024]{1,0:T(8,128)(2,1)S(1)} %get-tuple-element.270, f32[64,2048]{1,0:T(8,128)S(1)} %get-tuple-element.282, pred[]{:T(512)S(6)} %compare.11, bf16[64,6144]{1,0:T(8,128)(2,1)} %get-tuple-element.293, s32[]{:T(128)S(6)} %select_n.276), kind=kOutput, calls=%fused_computation.25.clone.1 | convolution fusion | flops 277086208 | bytes 5373957 | tf_op jit(solution)/shard_map/while/body/eval_jaxpr/dot_general | solution.py:103
  70.6 20.5 %fusion.74 = (bf16[1024,1024]{1,0:T(8,128)(2,1)S(1)}, bf16[1024,1024]{1,0:T(8,128)(2,1)}) fusion(s32[1024]{0:T(1024)} %get-tuple-element.296, f32[1024]{0:T(1024)S(1)} %bitcast.91, f32[1024]{0:T(1024)S(1)} %bitcast.92), kind=kLoop, calls=%fused_computation.20.clone.1 | loop fusion | flops 19922944 | bytes 4206592 | tf_op jit(solution)/shard_map/convert
  91.0 2.6 %fusion.75 = f32[64,2048]{1,0:T(8,128)S(1)} fusion(bf16[1024,1024]{1,0:T(8,128)(2,1)} %get-tuple-element.269, bf16[1024,1024]{1,0:T(8,128)(2,1)S(1)} %get-tuple-element.270, f32[64,2048]{1,0:T(8,128)S(1)} %get-tuple-element.282, pred[]{:T(512)S(6)} %compare.11, bf16[64,6144]{1,0:T(8,128)(2,1)} %get-tuple-element.293, s32[]{:T(128)S(6)} %select_n.276), kind=kOutput, calls=%fused_computation.25.clone.1 | convolution fusion | flops 277086208 | bytes 5373957 | tf_op jit(solution)/shard_map/while/body/eval_jaxpr/dot_general | solution.py:103
  93.7 20.5 %fusion.74 = (bf16[1024,1024]{1,0:T(8,128)(2,1)S(1)}, bf16[1024,1024]{1,0:T(8,128)(2,1)}) fusion(s32[1024]{0:T(1024)} %get-tuple-element.296, f32[1024]{0:T(1024)S(1)} %bitcast.91, f32[1024]{0:T(1024)S(1)} %bitcast.92), kind=kLoop, calls=%fused_computation.20.clone.1 | loop fusion | flops 19922944 | bytes 4206592 | tf_op jit(solution)/shard_map/convert
  114.2 2.6 %fusion.75 = f32[64,2048]{1,0:T(8,128)S(1)} fusion(bf16[1024,1024]{1,0:T(8,128)(2,1)} %get-tuple-element.269, bf16[1024,1024]{1,0:T(8,128)(2,1)S(1)} %get-tuple-element.270, f32[64,2048]{1,0:T(8,128)S(1)} %get-tuple-element.282, pred[]{:T(512)S(6)} %compare.11, bf16[64,6144]{1,0:T(8,128)(2,1)} %get-tuple-element.293, s32[]{:T(128)S(6)} %select_n.276), kind=kOutput, calls=%fused_computation.25.clone.1 | convolution fusion | flops 277086208 | bytes 5373957 | tf_op jit(solution)/shard_map/while/body/eval_jaxpr/dot_general | solution.py:103
  116.8 20.5 %fusion.74 = (bf16[1024,1024]{1,0:T(8,128)(2,1)S(1)}, bf16[1024,1024]{1,0:T(8,128)(2,1)}) fusion(s32[1024]{0:T(1024)} %get-tuple-element.296, f32[1024]{0:T(1024)S(1)} %bitcast.91, f32[1024]{0:T(1024)S(1)} %bitcast.92), kind=kLoop, calls=%fused_computation.20.clone.1 | loop fusion | flops 19922944 | bytes 4206592 | tf_op jit(solution)/shard_map/convert
  137.3 2.6 %fusion.75 = f32[64,2048]{1,0:T(8,128)S(1)} fusion(bf16[1024,1024]{1,0:T(8,128)(2,1)} %get-tuple-element.269, bf16[1024,1024]{1,0:T(8,128)(2,1)S(1)} %get-tuple-element.270, f32[64,2048]{1,0:T(8,128)S(1)} %get-tuple-element.282, pred[]{:T(512)S(6)} %compare.11, bf16[64,6144]{1,0:T(8,128)(2,1)} %get-tuple-element.293, s32[]{:T(128)S(6)} %select_n.276), kind=kOutput, calls=%fused_computation.25.clone.1 | convolution fusion | flops 277086208 | bytes 5373957 | tf_op jit(solution)/shard_map/while/body/eval_jaxpr/dot_general | solution.py:103
  141.4 1.6 collective-permute-start.1
  144.5 2.1 collective-permute-done
  156.3 2.3 %copy.23 = f32[256,32,8,2]{1,3,2,0:T(2,128)} copy(f32[256,32,8,2]{0,1,3,2:T(8,128)S(1)} %maximum_bitcast_fusion.1) | data formatting | bytes 1048576 | tf_op jit(solution)/shard_map/transpose | solution.py:66
  160.1 5.6 %collective-permute-done.3 = f32[8,32,2,256]{3,1,2,0:T(8,128)} collective-permute-done((f32[8,32,2,256]{3,1,2,0:T(8,128)S(1)}, f32[8,32,2,256]{3,1,2,0:T(8,128)}, u32[]{:S(2)}, u32[]{:S(2)}) %collective-permute-start.3) | collective-permute-done | bytes 524320 | tf_op jit(solution)/shard_map/ppermute | solution.py:31
  165.7 3.9 %copy.24 = f32[256,32,8,2]{1,3,2,0:T(2,128)} copy(f32[256,32,8,2]{0,1,3,2:T(8,128)} %bitcast.13) | data formatting | bytes 1048576 | tf_op jit(solution)/shard_map/transpose | solution.py:66
  169.6 7.1 %collective-permute-done.4 = f32[8,32,2,256]{3,1,2,0:T(8,128)S(1)} collective-permute-done((f32[8,32,2,256]{3,1,2,0:T(8,128)S(1)}, f32[8,32,2,256]{3,1,2,0:T(8,128)S(1)}, u32[]{:S(2)}, u32[]{:S(2)}) %collective-permute-start.4) | collective-permute-done | bytes 524320 | tf_op jit(solution)/shard_map/ppermute | solution.py:31
  176.8 2.4 %copy.25 = f32[256,32,8,2]{1,3,2,0:T(2,128)} copy(f32[256,32,8,2]{0,1,3,2:T(8,128)S(1)} %bitcast.90) | data formatting | bytes 1048576 | tf_op jit(solution)/shard_map/transpose | solution.py:66
  179.1 18.9 %broadcast_multiply_fusion = f32[256,64,96]{2,1,0:T(8,128)} fusion(f32[256,32,16]{1,2,0:T(8,128)} %bitcast.81, f32[256,32,16]{1,2,0:T(8,128)S(1)} %bitcast.80, f32[256,32,16]{1,2,0:T(8,128)} %bitcast.83, f32[256,32,16]{1,2,0:T(8,128)} %bitcast.82), kind=kOutput, calls=%fused_computation.32 | convolution fusion | flops 304611328 | bytes 8388608 | tf_op jit(solution)/shard_map/fik,fjk->fij/dot_general | solution.py:76
  198.1 8.5 %copy.26 = f32[256,64,96]{0,2,1:T(8,128)} copy(f32[256,64,96]{2,1,0:T(8,128)} %broadcast_multiply_fusion) | data formatting | bytes 12582912 | tf_op jit(solution)/shard_map/div | solution.py:76
  206.6 3.7 %select_bitcast_fusion = f32[1,256,2,32,32]{1,4,3,2,0:T(8,128)S(1)} fusion(f32[256,2,32,3,32]{0,4,3,2,1:T(8,128)} %bitcast.78, pred[]{:T(512)} %bitcast.27, pred[]{:T(512)} %bitcast.25), kind=kLoop, calls=%fused_computation.51 | loop fusion | flops 1048576 | bytes 8388610 | tf_op jit(solution)/shard_map/jit(_where)/select_n | solution.py:82
  213.1 3.5 %copy.33 = f32[32,3,2,32,256]{4,3,2,1,0:T(8,128)} copy(f32[32,3,2,32,256]{4,3,0,2,1:T(8,128)S(1)} %maximum_bitcast_fusion) | data formatting | bytes 12582912 | tf_op jit(solution)/shard_map/transpose | solution.py:89
  (39 shorter events, 14.3 us)
Async XLA Ops:
  140.8 11.0 %copy-start.1 = (s32[1,3]{1,0:T(1,128)S(1)}, s32[1,3]{1,0:T(1,128)}, u32[]{:S(2)}) copy-start(s32[1,3]{1,0:T(1,128)} %param.6) | copy-start | bytes 40
  141.4 5.2 %collective-permute-start = (f32[1,2,32,2,256]{4,2,3,1,0:T(8,128)S(1)}, f32[1,2,32,2,256]{4,2,3,1,0:T(8,128)S(1)}, u32[]{:S(2)}, u32[]{:S(2)}) collective-permute-start(f32[1,2,32,2,256]{4,2,3,1,0:T(8,128)S(1)} %get-tuple-element.217), channel_id=1, source_target_pairs={{0,1},{1,2},{2,3},{3,0},{4,5},{5,6},{6,7},{7,4},{8,9},{9,10},{10,1... | collective-permute-start | bytes 393224 | tf_op jit(solution)/shard_map/ppermute | solution.py:123
  141.4 6.4 %collective-permute-start.1 = (f32[1,2,32,2,256]{4,2,3,1,0:T(8,128)S(1)}, f32[1,2,32,2,256]{4,2,3,1,0:T(8,128)S(1)}, u32[]{:S(2)}, u32[]{:S(2)}) collective-permute-start(f32[1,2,32,2,256]{4,2,3,1,0:T(8,128)S(1)} %get-tuple-element.216), channel_id=1, source_target_pairs={{0,2},{1,3},{2,0},{3,1},{4,6},{5,7},{6,4},{7,5},{8,10},{9,11},{10,... | collective-permute-start | bytes 393224 | tf_op jit(solution)/shard_map/ppermute | solution.py:123
  143.0 6.0 %collective-permute-start.2 = (f32[1,2,32,2,256]{4,2,3,1,0:T(8,128)S(1)}, f32[1,2,32,2,256]{4,2,3,1,0:T(8,128)S(1)}, u32[]{:S(2)}, u32[]{:S(2)}) collective-permute-start(f32[1,2,32,2,256]{4,2,3,1,0:T(8,128)S(1)} %get-tuple-element.215), channel_id=1, source_target_pairs={{0,3},{1,0},{2,1},{3,2},{4,7},{5,4},{6,5},{7,6},{8,11},{9,8},{10,9... | collective-permute-start | bytes 393224 | tf_op jit(solution)/shard_map/ppermute | solution.py:123
  149.1 16.6 %collective-permute-start.3 = (f32[8,32,2,256]{3,1,2,0:T(8,128)S(1)}, f32[8,32,2,256]{3,1,2,0:T(8,128)}, u32[]{:S(2)}, u32[]{:S(2)}) collective-permute-start(f32[8,32,2,256]{3,1,2,0:T(8,128)S(1)} %bitcast.84), channel_id=1, source_target_pairs={{0,4},{4,8},{8,12},{12,16},{16,20},{20,24},{24,28},{1,5},{5,9},{9,... | collective-permute-start | bytes 1572872 | tf_op jit(solution)/shard_map/ppermute | solution.py:31
  150.4 26.4 %collective-permute-start.4 = (f32[8,32,2,256]{3,1,2,0:T(8,128)S(1)}, f32[8,32,2,256]{3,1,2,0:T(8,128)S(1)}, u32[]{:S(2)}, u32[]{:S(2)}) collective-permute-start(f32[8,32,2,256]{3,1,2,0:T(8,128)S(1)} %bitcast.85), channel_id=1, source_target_pairs={{0,8},{4,12},{8,16},{12,20},{16,24},{20,28},{1,9},{5,13},{9,17},{1... | collective-permute-start | bytes 1572872 | tf_op jit(solution)/shard_map/ppermute | solution.py:31
  206.6 4.7 %copy-start = (f32[256,64,96]{0,2,1:T(8,128)S(1)}, f32[256,64,96]{0,2,1:T(8,128)}, u32[]{:S(2)}) copy-start(f32[256,64,96]{0,2,1:T(8,128)} %copy.26) | copy-start | bytes 18874372
